TPU v7x, 32 devices: a whole 2x2x4 slice. The times are simulated.
32 devices in a mesh: groups: 2 (over y), strip: 4 (over z), section: 2 (over x), col: 2 (over core).
Axes of the slice: x: 2, y: 2, z: 4, core: 2. Of those that a mesh axis runs over, the one named last changes fastest.
Arguments:
- x_in: float32 [8, 512, 16, 256], P('groups', None, 'strip', 'col'), parts along dimension 0, may hold values from -6 to 6
- w_reduce: float32 [2, 128, 512], P('section'), may hold values from -0.25 to 0.25
- w_spatial: float32 [2, 9, 128, 128], P('section'), may hold values from -0.1875 to 0.1875
- w_expand: float32 [2, 512, 128], P('section'), may hold values from -0.5 to 0.5
- gain_mid: float32 [2, 2, 128], P('section'), may hold values from 0.1 to 1.9
- bias_mid: float32 [2, 2, 128], P('section'), may hold values from -3 to 3
- gain_out: float32 [2, 512], P('section'), may hold values from 0.1 to 1.9
- bias_out: float32 [2, 512], P('section'), may hold values from -3 to 3
Outputs:
- features: float32 [2, 8, 512, 16, 256], P('section', 'groups', None, 'strip', 'col'), parts along dimension 1
There are 2 independent parts, one for each index of `groups`. A program takes and returns all parts, laid end to end along the dimension named above; an argument that names none is the same for every part. Nothing has to cross between parts.
All inputs are finite; a program needn't handle non-finite values.
Results may differ from a plain program's by a relative error of at most 0.00015.
Values sent between devices are 32-bit elements; how exact they have to be, the bound alone decides.
A program may use at most 64 MiB of HBM per device.

v0:
```python
import functools

import jax
import jax.numpy as jnp
from jax import lax
from jax.experimental import pallas as pl
from jax.experimental.pallas import tpu as pltpu
from jax.sharding import PartitionSpec as P

BF = jnp.bfloat16
F32 = jnp.float32


def split(value):
    high = value.astype(BF)
    return high, (value - high.astype(F32)).astype(BF)


def dot(a, b):
    return jnp.dot(a, b, preferred_element_type=F32)


def down_rows(row, size):
    return jnp.transpose(jnp.broadcast_to(row, (size, size)))


def kernel(
    levels, strips, rows,
    x_ref, wr_ref, ws_ref, wx_ref, pp_ref, out_ref,
    cur, wr_all, ws_all, wx_all, pp_all, red, side, halo, relay,
    w_red, w_spa, w_exp, b_red, b_mid, b_out, sa,
    x_sem, own_sem, wsend, wrecv, rsend, rrecv, hsend, hrecv, nsend, nrecv, ysend, yrecv, out_sem,
):
    tiles = x_ref.shape[0]
    chans = x_ref.shape[1] // rows
    cols = x_ref.shape[2]
    mid = wr_ref.shape[0]
    strip = lax.axis_index("strip")
    sec = lax.axis_index("section")
    col = lax.axis_index("col")
    other = {"col": 1 - col}
    srcs = (wr_ref, ws_ref, wx_ref, pp_ref)
    slots = (wr_all, ws_all, wx_all, pp_all)

    def share(kind, level, which):
        if kind == 0:
            return wr_all.at[level, pl.ds(which * (mid // 2), mid // 2), :]
        if kind == 1:
            return ws_all.at[level, :, pl.ds(which * (mid // 2), mid // 2), :]
        if kind == 2:
            return wx_all.at[level, pl.ds(which * (chans // 2), chans // 2), :]
        return pp_all.at[level]

    def remote(src, dst, send, recv, device):
        return pltpu.make_async_remote_copy(
            src_ref=src, dst_ref=dst, send_sem=send, recv_sem=recv,
            device_id=device, device_id_type=pl.DeviceIdType.MESH,
        )

    own = [
        pltpu.make_async_copy(srcs[k], slots[k].at[sec], own_sem.at[k]) for k in range(4)
    ]
    loads = [
        pltpu.make_async_copy(x_ref.at[m], cur.at[m], x_sem.at[m]) for m in range(tiles)
    ]
    for copy in (own[3], own[0], own[1], own[2]):
        copy.start()
    for copy in loads:
        copy.start()

    barrier = pltpu.get_barrier_semaphore()
    pl.semaphore_signal(barrier, inc=1, device_id=other, device_id_type=pl.DeviceIdType.MESH)
    for step in range(1, levels):
        pl.semaphore_signal(
            barrier, inc=1, device_id={"section": lax.rem(sec + step, levels)},
            device_id_type=pl.DeviceIdType.MESH,
        )

    for there, peer in ((strip > 0, strip - 1), (strip < strips - 1, strip + 1)):
        @pl.when(there)
        def _(peer=peer):
            pl.semaphore_signal(
                barrier, inc=1, device_id={"strip": peer}, device_id_type=pl.DeviceIdType.MESH
            )

    peers = levels + jnp.where(strip > 0, 1, 0) + jnp.where(strip < strips - 1, 1, 0)
    pl.semaphore_wait(barrier, peers)

    for k in (3, 0, 1, 2):
        own[k].wait()
        for target in range(1, levels):
            @pl.when(sec < target)
            def _(k=k, target=target):
                part = share(k, sec, col)
                remote(part, part, wsend.at[k, target], wrecv.at[k, sec], {"section": target}).start()

    @pl.when(strip == 0)
    def _():
        halo[:, :, 0] = jnp.zeros(halo.shape[:2] + halo.shape[3:], F32)
        relay[:, :, 0] = jnp.zeros(relay.shape[:2] + relay.shape[3:], F32)

    @pl.when(strip == strips - 1)
    def _():
        halo[:, :, 1] = jnp.zeros(halo.shape[:2] + halo.shape[3:], F32)
        relay[:, :, 1] = jnp.zeros(relay.shape[:2] + relay.shape[3:], F32)

    def relayed(k, level, which):
        part = share(k, level, which)
        return remote(part, part, rsend.at[k, level], rrecv.at[k, level], other)

    def arrive(level, kinds):
        @pl.when(sec > level)
        def _():
            for k in kinds:
                part = share(k, level, col)
                remote(part, part, wsend.at[k, 0], wrecv.at[k, level], other).wait_recv()
                if k < 3:
                    relayed(k, level, col).start()
            for k in kinds:
                if k < 3:
                    relayed(k, level, 1 - col).wait_recv()

    def prepare_reduce(level):
        arrive(level, (3, 0))
        gain = down_rows(pp_all[level, 0:1, :], mid)
        for at in range(chans // mid):
            cut = slice(at * mid, (at + 1) * mid)
            high, low = split(wr_all[level, :, cut] * gain)
            w_red[level, 0:mid, cut] = high
            w_red[level, mid : 2 * mid, cut] = low
        b_red[level] = down_rows(pp_all[level, 2:3, :], mid)

    def prepare_rest(level):
        arrive(level, (1, 2))
        gain = down_rows(pp_all[level, 1:2, :], mid)
        for tap in range(9):
            p, q = tap // 3, tap % 3
            high, low = split(ws_all[level, tap] * gain)
            w_spa[p, 0:mid, q * mid : (q + 1) * mid] = high
            w_spa[p, mid : 2 * mid, q * mid : (q + 1) * mid] = low
        b_mid[...] = down_rows(pp_all[level, 3:4, :], mid)
        count = chans // mid
        for at in range(count):
            cut = slice(at * mid, (at + 1) * mid)
            high, low = split(wx_all[level, cut, :] * down_rows(pp_all[level, 4 + at : 5 + at, :], mid))
            w_exp[cut, 0:mid] = high
            w_exp[cut, mid : 2 * mid] = high
            w_exp[cut, 2 * mid : 3 * mid] = low
            b_out[cut, :] = down_rows(pp_all[level, 4 + count + at : 5 + count + at, :], mid)

    def to_strip(level, m, way):
        return remote(
            red.at[level, m, rows - 1 if way == 0 else 0], halo.at[level, m, way],
            hsend.at[level, m, way], hrecv.at[level, m, way],
            {"strip": strip + 1 if way == 0 else strip - 1},
        )

    def to_side(level, m):
        return remote(red.at[level, m], side.at[level, m], nsend.at[level, m], nrecv.at[level, m], other)

    def pass_on(level, m, way):
        return remote(
            halo.at[level, m, way], relay.at[level, m, way],
            ysend.at[level, m, way], yrecv.at[level, m, way], other,
        )

    has = (strip > 0, strip < strips - 1)

    def reduce_tile(level, m):
        weights = w_red[level]
        bias = b_red[level]
        for pair in range(rows // 2):
            parts = [
                split(cur.at[m][pl.ds(2 * pair + j, chans, stride=rows), :]) for j in range(2)
            ]
            high = jnp.concatenate([part[0] for part in parts], axis=1)
            low = jnp.concatenate([part[1] for part in parts], axis=1)
            both = dot(weights, high)
            total = both[:mid] + both[mid:] + dot(weights[:mid], low)
            for j in range(2):
                red[level, m, 2 * pair + j] = jnp.maximum(total[:, j * cols : (j + 1) * cols] + bias, 0.0)

        @pl.when(has[1])
        def _():
            to_strip(level, m, 0).start()

        @pl.when(has[0])
        def _():
            to_strip(level, m, 1).start()

        to_side(level, m).start()

    def take_halo(level, m):
        for way in range(2):
            @pl.when(has[way])
            def _(way=way):
                to_strip(level, m, way).wait_recv()
                pass_on(level, m, way).start()

    lane = lax.broadcasted_iota(jnp.int32, (mid, cols), 1)
    left_edge = lane == cols - 1
    right_edge = lane == 0
    left_on = jnp.where(col == 1, 1.0, 0.0).astype(F32)
    right_on = jnp.where(col == 0, 1.0, 0.0).astype(F32)

    def finish_tile(level, m):
        to_side(level, m).wait_recv()
        for way in range(2):
            @pl.when(has[way])
            def _(way=way):
                pass_on(level, m, way).wait_recv()
        for at in range(rows + 2):
            if at == 0:
                centre, beside = halo[level, m, 0], relay[level, m, 0]
            elif at == rows + 1:
                centre, beside = halo[level, m, 1], relay[level, m, 1]
            else:
                centre, beside = red[level, m, at - 1], side[level, m, at - 1]
            lanes = slice(at * cols, (at + 1) * cols)
            left = pltpu.roll(jnp.where(left_edge, beside * left_on, centre), 1, 1)
            right = pltpu.roll(jnp.where(right_edge, beside * right_on, centre), cols - 1, 1)
            for q, value in enumerate((left, centre, right)):
                high, low = split(value)
                sa[q * mid : (q + 1) * mid, lanes] = high
                sa[(3 + q) * mid : (4 + q) * mid, lanes] = low
        bias = b_mid[...]
        for pair in range(rows // 2):
            both = jnp.zeros((2 * mid, 2 * cols), F32)
            one = jnp.zeros((mid, 2 * cols), F32)
            for p in range(3):
                lanes = slice((2 * pair + p) * cols, (2 * pair + p + 2) * cols)
                both = both + dot(w_spa[p], sa[0 : 3 * mid, lanes])
                one = one + dot(w_spa[p, 0:mid, :], sa[3 * mid : 6 * mid, lanes])
            total = both[:mid] + both[mid:] + one
            total = jnp.maximum(total + jnp.concatenate([bias, bias], axis=1), 0.0)
            high, low = split(total)
            stack = jnp.concatenate([high, low, high], axis=0)
            grown = dot(w_exp[...], stack)
            for j in range(2):
                at = pl.ds(2 * pair + j, chans, stride=rows)
                cur.at[m][at, :] = jnp.maximum(
                    cur.at[m][at, :] + grown[:, j * cols : (j + 1) * cols] + b_out[...], 0.0
                )

    def store(m):
        return pltpu.make_async_copy(cur.at[m], out_ref.at[m], out_sem.at[m])

    prepare_reduce(0)

    @pl.loop(0, tiles)
    def _(m):
        pltpu.make_async_copy(x_ref.at[m], cur.at[m], x_sem.at[m]).wait()
        reduce_tile(0, m)

    for level in range(levels):
        @pl.when(sec >= level)
        def _(level=level):
            prepare_rest(level)
            if level + 1 < levels:
                @pl.when(sec > level)
                def _():
                    prepare_reduce(level + 1)

            take_halo(level, 0)

            @pl.loop(0, tiles)
            def _(m):
                @pl.when(m + 1 < tiles)
                def _():
                    take_halo(level, m + 1)

                finish_tile(level, m)
                if level + 1 < levels:
                    @pl.when(sec > level)
                    def _():
                        reduce_tile(level + 1, m)

                @pl.when(sec == level)
                def _():
                    store(m).start()

            @pl.loop(0, tiles)
            def _(m):
                to_side(level, m).wait_send()
                for way in range(2):
                    @pl.when(has[1 - way])
                    def _(way=way):
                        to_strip(level, m, way).wait_send()

                    @pl.when(has[way])
                    def _(way=way):
                        pass_on(level, m, way).wait_send()

                @pl.when(sec == level)
                def _():
                    store(m).wait()

    for k in range(4):
        for target in range(1, levels):
            @pl.when(sec < target)
            def _(k=k, target=target):
                part = share(k, sec, col)
                remote(part, part, wsend.at[k, target], wrecv.at[k, sec], {"section": target}).wait_send()
        if k < 3:
            for level in range(levels - 1):
                @pl.when(sec > level)
                def _(k=k, level=level):
                    relayed(k, level, col).wait_send()


def on_device(levels, strips, x_in, w_reduce, w_spatial, w_expand, gain_mid, bias_mid, gain_out, bias_out):
    tiles, chans, rows, cols = x_in.shape
    mid = w_reduce.shape[1]
    terms = jnp.concatenate(
        [
            gain_mid[0], bias_mid[0],
            gain_out.reshape(chans // mid, mid), bias_out.reshape(chans // mid, mid),
            jnp.zeros((4, mid), F32),
        ],
        axis=0,
    )
    dma = pltpu.SemaphoreType.DMA
    out = pl.pallas_call(
        functools.partial(kernel, levels, strips, rows),
        out_shape=jax.ShapeDtypeStruct((tiles, chans * rows, cols), F32),
        in_specs=[pl.BlockSpec(memory_space=pl.ANY)] * 5,
        out_specs=pl.BlockSpec(memory_space=pl.ANY),
        scratch_shapes=[
            pltpu.VMEM((tiles, chans * rows, cols), F32),
            pltpu.VMEM((levels, mid, chans), F32),
            pltpu.VMEM((levels, 9, mid, mid), F32),
            pltpu.VMEM((levels, chans, mid), F32),
            pltpu.VMEM((levels,) + terms.shape, F32),
            pltpu.VMEM((levels, tiles, rows, mid, cols), F32),
            pltpu.VMEM((levels, tiles, rows, mid, cols), F32),
            pltpu.VMEM((levels, tiles, 2, mid, cols), F32),
            pltpu.VMEM((levels, tiles, 2, mid, cols), F32),
            pltpu.VMEM((levels, 2 * mid, chans), BF),
            pltpu.VMEM((3, 2 * mid, 3 * mid), BF),
            pltpu.VMEM((chans, 3 * mid), BF),
            pltpu.VMEM((levels, mid, cols), F32),
            pltpu.VMEM((mid, cols), F32),
            pltpu.VMEM((chans, cols), F32),
            pltpu.VMEM((6 * mid, (rows + 2) * cols), BF),
            dma((tiles,)),
            dma((4,)),
            dma((4, levels)),
            dma((4, levels)),
            dma((3, levels)),
            dma((3, levels)),
            dma((levels, tiles, 2)),
            dma((levels, tiles, 2)),
            dma((levels, tiles)),
            dma((levels, tiles)),
            dma((levels, tiles, 2)),
            dma((levels, tiles, 2)),
            dma((tiles,)),
        ],
        compiler_params=pltpu.CompilerParams(
            collective_id=0, has_side_effects=True, vmem_limit_bytes=60 * 1024 * 1024
        ),
        name="blocks",
    )(x_in.reshape(tiles, chans * rows, cols), w_reduce[0], w_spatial[0], w_expand[0], terms)
    return out.reshape(1, tiles, chans, rows, cols)


def solution(mesh):
    in_specs = (
        P("groups", None, "strip", "col"),
        P("section", None, None),
        P("section", None, None, None),
        P("section", None, None),
        P("section", None, None),
        P("section", None, None),
        P("section", None),
        P("section", None),
    )
    out_specs = P("section", "groups", None, "strip", "col")
    return jax.shard_map(
        functools.partial(on_device, mesh.shape["section"], mesh.shape["strip"]),
        mesh=mesh, in_specs=in_specs, out_specs=out_specs, check_vma=False,
    )
```

profile of v0, /device:TPU:19, one launch (start us, length us, event | category | flops | bytes accessed | tf_op | source)
XLA Modules:
  0.0 48.3 jit_solution(7969270029403871171)
XLA Ops:
  0.0 2.6 %concatenate.3.pp_ref = f32[16,128]{1,0:T(8,128)} concatenate(f32[2,128]{1,0:T(2,128)} %bitcast.16, f32[2,128]{1,0:T(2,128)} %bitcast.17, f32[4,128]{1,0:T(4,128)} %bitcast.14, f32[4,128]{1,0:T(4,128)} %bitcast.15, f32[4,128]{1,0:T(4,128)S(1)} %broadcast_in_dim.3), dimensions={0} | concatenate | bytes 16384 | tf_op jit(solution)/shard_map/concatenate | solution.py:314
  2.6 41.2 %blocks.1 = f32[4,2048,128]{2,1,0:T(8,128)} custom-call(f32[4,2048,128]{2,1,0:T(8,128)} %bitcast.10, f32[128,512]{1,0:T(8,128)} %bitcast.12, f32[9,128,128]{2,1,0:T(8,128)} %bitcast.11, f32[512,128]{1,0:T(8,128)} %bitcast.13, f32[16,128]{1,0:T(8,128)} %concatenate.3.pp_ref), custom_call_target="tpu_custom_call" | custom-call | tf_op jit(solution)/shard_map/blocks/pallas_call | solution.py:323
  43.8 4.5 %copy.10 = f32[1,4,512,4,128]{4,3,2,1,0:T(4,128)} copy(f32[1,4,512,4,128]{4,3,2,1,0:T(4,128)} %bitcast.9) | data formatting | bytes 8388608
  (1 shorter events, 0.0 us)
where the time goes:
time: 48.5 us; the launch traced here: 48.3 us
  Pallas kernels  41.2 us (85%)
  local copies, waits for them, and re-layouts  7.07 us (15%)
    pallas_call x1, Pallas kernels, on_device(): pl.pallas_call(functools.partial(kernel, levels, strips, rows), out_shape...  41.2 us
    unnamed x1, local copies, waits for them, and re-layouts  4.47 us
    concatenate x1, local copies, waits for them, and re-layouts, on_device(): jnp.concatenate([gain_mid[0], bias_mid[0], gain_out.reshape(chans // mid,...  2.6 us

commit v1 on v0

--- a/solution.py
+++ b/solution.py
@@ -26,10 +26,10 @@
 
 def kernel(
     levels, strips, rows,
-    x_ref, wr_ref, ws_ref, wx_ref, pp_ref, out_ref,
-    cur, wr_all, ws_all, wx_all, pp_all, red, side, halo, relay,
+    x_ref, wr_ref, ws_ref, wx_ref, gm_ref, bm_ref, go_ref, bo_ref, cur,
+    wr_all, ws_all, wx_all, pp_all, red, side, halo, relay,
     w_red, w_spa, w_exp, b_red, b_mid, b_out, sa,
-    x_sem, own_sem, wsend, wrecv, rsend, rrecv, hsend, hrecv, nsend, nrecv, ysend, yrecv, out_sem,
+    x_sem, own_sem, wsend, wrecv, rsend, rrecv, hsend, hrecv, nsend, nrecv, ysend, yrecv,
 ):
     tiles = x_ref.shape[0]
     chans = x_ref.shape[1] // rows
@@ -39,7 +39,9 @@
     sec = lax.axis_index("section")
     col = lax.axis_index("col")
     other = {"col": 1 - col}
-    srcs = (wr_ref, ws_ref, wx_ref, pp_ref)
+    srcs = (wr_ref, ws_ref, wx_ref)
+    count = chans // mid
+    terms = ((gm_ref, 0, 2), (bm_ref, 2, 2), (go_ref, 4, count), (bo_ref, 4 + count, count))
     slots = (wr_all, ws_all, wx_all, pp_all)
 
     def share(kind, level, which):
@@ -58,12 +60,17 @@
         )
 
     own = [
-        pltpu.make_async_copy(srcs[k], slots[k].at[sec], own_sem.at[k]) for k in range(4)
+        pltpu.make_async_copy(srcs[k], slots[k].at[sec], own_sem.at[k]) for k in range(3)
+    ] + [
+        [
+            pltpu.make_async_copy(src, pp_all.at[sec, pl.ds(first, size), :], own_sem.at[3 + i])
+            for i, (src, first, size) in enumerate(terms)
+        ]
     ]
     loads = [
         pltpu.make_async_copy(x_ref.at[m], cur.at[m], x_sem.at[m]) for m in range(tiles)
     ]
-    for copy in (own[3], own[0], own[1], own[2]):
+    for copy in (*own[3], own[0], own[1], own[2]):
         copy.start()
     for copy in loads:
         copy.start()
@@ -87,7 +94,8 @@
     pl.semaphore_wait(barrier, peers)
 
     for k in (3, 0, 1, 2):
-        own[k].wait()
+        for copy in own[3] if k == 3 else (own[k],):
+            copy.wait()
         for target in range(1, levels):
             @pl.when(sec < target)
             def _(k=k, target=target):
@@ -139,7 +147,6 @@
             w_spa[p, 0:mid, q * mid : (q + 1) * mid] = high
             w_spa[p, mid : 2 * mid, q * mid : (q + 1) * mid] = low
         b_mid[...] = down_rows(pp_all[level, 3:4, :], mid)
-        count = chans // mid
         for at in range(count):
             cut = slice(at * mid, (at + 1) * mid)
             high, low = split(wx_all[level, cut, :] * down_rows(pp_all[level, 4 + at : 5 + at, :], mid))
@@ -242,9 +249,6 @@
                     cur.at[m][at, :] + grown[:, j * cols : (j + 1) * cols] + b_out[...], 0.0
                 )
 
-    def store(m):
-        return pltpu.make_async_copy(cur.at[m], out_ref.at[m], out_sem.at[m])
-
     prepare_reduce(0)
 
     @pl.loop(0, tiles)
@@ -275,10 +279,6 @@
                     def _():
                         reduce_tile(level + 1, m)
 
-                @pl.when(sec == level)
-                def _():
-                    store(m).start()
-
             @pl.loop(0, tiles)
             def _(m):
                 to_side(level, m).wait_send()
@@ -290,10 +290,6 @@
                     @pl.when(has[way])
                     def _(way=way):
                         pass_on(level, m, way).wait_send()
-
-                @pl.when(sec == level)
-                def _():
-                    store(m).wait()
 
     for k in range(4):
         for target in range(1, levels):
@@ -311,26 +307,17 @@
 def on_device(levels, strips, x_in, w_reduce, w_spatial, w_expand, gain_mid, bias_mid, gain_out, bias_out):
     tiles, chans, rows, cols = x_in.shape
     mid = w_reduce.shape[1]
-    terms = jnp.concatenate(
-        [
-            gain_mid[0], bias_mid[0],
-            gain_out.reshape(chans // mid, mid), bias_out.reshape(chans // mid, mid),
-            jnp.zeros((4, mid), F32),
-        ],
-        axis=0,
-    )
     dma = pltpu.SemaphoreType.DMA
     out = pl.pallas_call(
         functools.partial(kernel, levels, strips, rows),
         out_shape=jax.ShapeDtypeStruct((tiles, chans * rows, cols), F32),
-        in_specs=[pl.BlockSpec(memory_space=pl.ANY)] * 5,
-        out_specs=pl.BlockSpec(memory_space=pl.ANY),
+        in_specs=[pl.BlockSpec(memory_space=pl.ANY)] * 8,
+        out_specs=pl.BlockSpec(memory_space=pltpu.VMEM),
         scratch_shapes=[
-            pltpu.VMEM((tiles, chans * rows, cols), F32),
             pltpu.VMEM((levels, mid, chans), F32),
             pltpu.VMEM((levels, 9, mid, mid), F32),
             pltpu.VMEM((levels, chans, mid), F32),
-            pltpu.VMEM((levels,) + terms.shape, F32),
+            pltpu.VMEM((levels, 4 + 2 * (chans // mid), mid), F32),
             pltpu.VMEM((levels, tiles, rows, mid, cols), F32),
             pltpu.VMEM((levels, tiles, rows, mid, cols), F32),
             pltpu.VMEM((levels, tiles, 2, mid, cols), F32),
@@ -343,7 +330,7 @@
             pltpu.VMEM((chans, cols), F32),
             pltpu.VMEM((6 * mid, (rows + 2) * cols), BF),
             dma((tiles,)),
-            dma((4,)),
+            dma((7,)),
             dma((4, levels)),
             dma((4, levels)),
             dma((3, levels)),
@@ -354,13 +341,13 @@
             dma((levels, tiles)),
             dma((levels, tiles, 2)),
             dma((levels, tiles, 2)),
-            dma((tiles,)),
         ],
         compiler_params=pltpu.CompilerParams(
-            collective_id=0, has_side_effects=True, vmem_limit_bytes=60 * 1024 * 1024
+            collective_id=0, has_side_effects=True, vmem_limit_bytes=40 * 1024 * 1024
         ),
         name="blocks",
-    )(x_in.reshape(tiles, chans * rows, cols), w_reduce[0], w_spatial[0], w_expand[0], terms)
+    )(x_in.reshape(tiles, chans * rows, cols), w_reduce[0], w_spatial[0], w_expand[0],
+      gain_mid[0], bias_mid[0], gain_out.reshape(chans // mid, mid), bias_out.reshape(chans // mid, mid))
     return out.reshape(1, tiles, chans, rows, cols)
 
 

time: 48.5 us -> 50.9 us (1.049)
  local copies, waits for them, and re-layouts: 7.07 us -> 9.88 us
    unnamed x1 -> x17, local copies, waits for them, and re-layouts: 4.47 us -> 9.88 us
    concatenate x1 -> x0, local copies, waits for them, and re-layouts: 2.6 us -> none  [on_device(): jnp.concatenate([gain_mid[0], bias_mid[0], gain_out.reshape(chans // mid,...]
    pallas_call x1, Pallas kernels: 41.2 us -> 40.7 us  [on_device(): pl.pallas_call(functools.partial(kernel, levels, strips, rows), out_shape...]
where the time goes in v1:
time: 50.9 us; the launch traced here: 50.6 us
  Pallas kernels  40.7 us (80%)
  local copies, waits for them, and re-layouts  9.88 us (19%)
    pallas_call x1, Pallas kernels, on_device(): pl.pallas_call(functools.partial(kernel, levels, strips, rows), out_shape...  40.7 us
    unnamed x17, local copies, waits for them, and re-layouts  9.88 us

profile of v1, /device:TPU:19, one launch (start us, length us, event | category | flops | bytes accessed | tf_op | source)
XLA Modules:
  0.0 50.6 jit_solution(12885940806417693491)
XLA Ops:
  0.0 0.0 copy-start
  0.0 2.2 %copy-done = f32[4,512,4,128]{3,2,1,0:T(4,128)S(1)} copy-done((f32[4,512,4,128]{3,2,1,0:T(4,128)S(1)}, f32[4,512,4,128]{3,2,1,0:T(4,128)}, u32[]{:S(2)}) %copy-start) | copy-done | bytes 4194328
  2.2 0.0 copy-start.1
  2.2 1.1 %copy-done.1 = f32[1,9,128,128]{3,2,1,0:T(8,128)S(1)} copy-done((f32[1,9,128,128]{3,2,1,0:T(8,128)S(1)}, f32[1,9,128,128]{3,2,1,0:T(8,128)}, u32[]{:S(2)}) %copy-start.1) | copy-done | bytes 589848
  3.3 0.0 copy-start.2
  3.3 0.9 %copy-done.2 = f32[1,128,512]{2,1,0:T(8,128)S(1)} copy-done((f32[1,128,512]{2,1,0:T(8,128)S(1)}, f32[1,128,512]{2,1,0:T(8,128)}, u32[]{:S(2)}) %copy-start.2) | copy-done | bytes 262168
  4.2 0.0 copy-start.3
  4.2 0.9 %copy-done.3 = f32[1,512,128]{2,1,0:T(8,128)S(1)} copy-done((f32[1,512,128]{2,1,0:T(8,128)S(1)}, f32[1,512,128]{2,1,0:T(8,128)}, u32[]{:S(2)}) %copy-start.3) | copy-done | bytes 262168
  5.2 0.0 copy-start.4
  5.2 0.7 %copy-done.4 = f32[1,512]{1,0:T(1,128)S(1)} copy-done((f32[1,512]{1,0:T(1,128)S(1)}, f32[1,512]{1,0:T(1,128)}, u32[]{:S(2)}) %copy-start.4) | copy-done | bytes 2072
  5.8 0.0 copy-start.5
  5.8 0.7 %copy-done.5 = f32[1,512]{1,0:T(1,128)S(1)} copy-done((f32[1,512]{1,0:T(1,128)S(1)}, f32[1,512]{1,0:T(1,128)}, u32[]{:S(2)}) %copy-start.5) | copy-done | bytes 2072
  6.5 0.0 copy-start.6
  6.5 0.7 %copy-done.6 = f32[1,2,128]{2,1,0:T(2,128)S(1)} copy-done((f32[1,2,128]{2,1,0:T(2,128)S(1)}, f32[1,2,128]{2,1,0:T(2,128)}, u32[]{:S(2)}) %copy-start.6) | copy-done | bytes 1048
  7.2 0.0 copy-start.7
  7.2 0.7 %copy-done.7 = f32[1,2,128]{2,1,0:T(2,128)S(1)} copy-done((f32[1,2,128]{2,1,0:T(2,128)S(1)}, f32[1,2,128]{2,1,0:T(2,128)}, u32[]{:S(2)}) %copy-start.7) | copy-done | bytes 1048
  7.9 40.7 %blocks.1 = f32[4,2048,128]{2,1,0:T(8,128)S(1)} custom-call(f32[4,2048,128]{2,1,0:T(8,128)S(1)} %bitcast.10, f32[128,512]{1,0:T(8,128)S(1)} %bitcast.12, f32[9,128,128]{2,1,0:T(8,128)S(1)} %bitcast.11, f32[512,128]{1,0:T(8,128)S(1)} %bitcast.13, f32[2,128]{1,0:T(2,128)S(1)} %bitcast.16, f32[2,128]{1,0:T(2,128)S(1)} %bitcast.17, f32[4,128]{1,0:T(4,128)S(1)} %bitcast.14, ...), custom_call_target="tpu_custom_call" | custom-call | tf_op jit(solution)/shard_map/blocks/pallas_call | solution.py:311
  48.6 2.0 %copy.10 = f32[1,4,512,4,128]{4,3,2,1,0:T(4,128)} copy(f32[1,4,512,4,128]{4,3,2,1,0:T(4,128)S(1)} %bitcast.9) | data formatting | bytes 8388608
Async XLA Ops:
  0.0 2.2 %copy-start = (f32[4,512,4,128]{3,2,1,0:T(4,128)S(1)}, f32[4,512,4,128]{3,2,1,0:T(4,128)}, u32[]{:S(2)}) copy-start(f32[4,512,4,128]{3,2,1,0:T(4,128)} %param.8) | copy-start | bytes 12582916
  2.2 1.1 %copy-start.1 = (f32[1,9,128,128]{3,2,1,0:T(8,128)S(1)}, f32[1,9,128,128]{3,2,1,0:T(8,128)}, u32[]{:S(2)}) copy-start(f32[1,9,128,128]{3,2,1,0:T(8,128)} %param.10) | copy-start | bytes 1769476
  3.3 0.9 %copy-start.2 = (f32[1,128,512]{2,1,0:T(8,128)S(1)}, f32[1,128,512]{2,1,0:T(8,128)}, u32[]{:S(2)}) copy-start(f32[1,128,512]{2,1,0:T(8,128)} %param.9) | copy-start | bytes 786436
  4.2 0.9 %copy-start.3 = (f32[1,512,128]{2,1,0:T(8,128)S(1)}, f32[1,512,128]{2,1,0:T(8,128)}, u32[]{:S(2)}) copy-start(f32[1,512,128]{2,1,0:T(8,128)} %param.11) | copy-start | bytes 786436
  5.2 0.7 %copy-start.4 = (f32[1,512]{1,0:T(1,128)S(1)}, f32[1,512]{1,0:T(1,128)}, u32[]{:S(2)}) copy-start(f32[1,512]{1,0:T(1,128)} %param.14) | copy-start | bytes 6148
  5.8 0.7 %copy-start.5 = (f32[1,512]{1,0:T(1,128)S(1)}, f32[1,512]{1,0:T(1,128)}, u32[]{:S(2)}) copy-start(f32[1,512]{1,0:T(1,128)} %param.15) | copy-start | bytes 6148
  6.5 0.7 %copy-start.6 = (f32[1,2,128]{2,1,0:T(2,128)S(1)}, f32[1,2,128]{2,1,0:T(2,128)}, u32[]{:S(2)}) copy-start(f32[1,2,128]{2,1,0:T(2,128)} %param.12) | copy-start | bytes 3076
  7.2 0.7 %copy-start.7 = (f32[1,2,128]{2,1,0:T(2,128)S(1)}, f32[1,2,128]{2,1,0:T(2,128)}, u32[]{:S(2)}) copy-start(f32[1,2,128]{2,1,0:T(2,128)} %param.13) | copy-start | bytes 3076

commit v2 on v1

--- a/solution.py
+++ b/solution.py
@@ -28,7 +28,7 @@
     levels, strips, rows,
     x_ref, wr_ref, ws_ref, wx_ref, gm_ref, bm_ref, go_ref, bo_ref, cur,
     wr_all, ws_all, wx_all, pp_all, red, side, halo, relay,
-    w_red, w_spa, w_exp, b_red, b_mid, b_out, sa,
+    w_red, w_spa, w_exp, b_red, b_mid, b_out, sa, middle,
     x_sem, own_sem, wsend, wrecv, rsend, rrecv, hsend, hrecv, nsend, nrecv, ysend, yrecv,
 ):
     tiles = x_ref.shape[0]
@@ -142,10 +142,9 @@
         arrive(level, (1, 2))
         gain = down_rows(pp_all[level, 1:2, :], mid)
         for tap in range(9):
-            p, q = tap // 3, tap % 3
             high, low = split(ws_all[level, tap] * gain)
-            w_spa[p, 0:mid, q * mid : (q + 1) * mid] = high
-            w_spa[p, mid : 2 * mid, q * mid : (q + 1) * mid] = low
+            w_spa[0:mid, tap * mid : (tap + 1) * mid] = high
+            w_spa[mid : 2 * mid, tap * mid : (tap + 1) * mid] = low
         b_mid[...] = down_rows(pp_all[level, 3:4, :], mid)
         for at in range(count):
             cut = slice(at * mid, (at + 1) * mid)
@@ -230,19 +229,23 @@
                 high, low = split(value)
                 sa[q * mid : (q + 1) * mid, lanes] = high
                 sa[(3 + q) * mid : (4 + q) * mid, lanes] = low
-        bias = b_mid[...]
+        wide = rows * cols
+        high, low = (
+            jnp.concatenate(
+                [sa[first : first + 3 * mid, p * cols : p * cols + wide] for p in range(3)], axis=0
+            )
+            for first in (0, 3 * mid)
+        )
+        both = dot(w_spa[...], high)
+        total = both[:mid] + both[mid:] + dot(w_spa[0:mid, :], low)
+        total = jnp.maximum(total + jnp.concatenate([b_mid[...]] * rows, axis=1), 0.0)
+        high, low = split(total)
+        middle[0:mid, :] = high
+        middle[mid : 2 * mid, :] = low
         for pair in range(rows // 2):
-            both = jnp.zeros((2 * mid, 2 * cols), F32)
-            one = jnp.zeros((mid, 2 * cols), F32)
-            for p in range(3):
-                lanes = slice((2 * pair + p) * cols, (2 * pair + p + 2) * cols)
-                both = both + dot(w_spa[p], sa[0 : 3 * mid, lanes])
-                one = one + dot(w_spa[p, 0:mid, :], sa[3 * mid : 6 * mid, lanes])
-            total = both[:mid] + both[mid:] + one
-            total = jnp.maximum(total + jnp.concatenate([bias, bias], axis=1), 0.0)
-            high, low = split(total)
-            stack = jnp.concatenate([high, low, high], axis=0)
-            grown = dot(w_exp[...], stack)
+            lanes = slice(2 * pair * cols, (2 * pair + 2) * cols)
+            high, low = middle[0:mid, lanes], middle[mid : 2 * mid, lanes]
+            grown = dot(w_exp[...], jnp.concatenate([high, low, high], axis=0))
             for j in range(2):
                 at = pl.ds(2 * pair + j, chans, stride=rows)
                 cur.at[m][at, :] = jnp.maximum(
@@ -307,11 +310,15 @@
 def on_device(levels, strips, x_in, w_reduce, w_spatial, w_expand, gain_mid, bias_mid, gain_out, bias_out):
     tiles, chans, rows, cols = x_in.shape
     mid = w_reduce.shape[1]
+    operands = (
+        x_in.reshape(tiles, chans * rows, cols), w_reduce[0], w_spatial[0], w_expand[0],
+        gain_mid[0], bias_mid[0], gain_out.reshape(chans // mid, mid), bias_out.reshape(chans // mid, mid),
+    )
     dma = pltpu.SemaphoreType.DMA
     out = pl.pallas_call(
         functools.partial(kernel, levels, strips, rows),
         out_shape=jax.ShapeDtypeStruct((tiles, chans * rows, cols), F32),
-        in_specs=[pl.BlockSpec(memory_space=pl.ANY)] * 8,
+        in_specs=[pl.BlockSpec(memory_space=pltpu.HBM)] * 8,
         out_specs=pl.BlockSpec(memory_space=pltpu.VMEM),
         scratch_shapes=[
             pltpu.VMEM((levels, mid, chans), F32),
@@ -323,12 +330,13 @@
             pltpu.VMEM((levels, tiles, 2, mid, cols), F32),
             pltpu.VMEM((levels, tiles, 2, mid, cols), F32),
             pltpu.VMEM((levels, 2 * mid, chans), BF),
-            pltpu.VMEM((3, 2 * mid, 3 * mid), BF),
+            pltpu.VMEM((2 * mid, 9 * mid), BF),
             pltpu.VMEM((chans, 3 * mid), BF),
             pltpu.VMEM((levels, mid, cols), F32),
             pltpu.VMEM((mid, cols), F32),
             pltpu.VMEM((chans, cols), F32),
             pltpu.VMEM((6 * mid, (rows + 2) * cols), BF),
+            pltpu.VMEM((2 * mid, rows * cols), BF),
             dma((tiles,)),
             dma((7,)),
             dma((4, levels)),
@@ -346,8 +354,7 @@
             collective_id=0, has_side_effects=True, vmem_limit_bytes=40 * 1024 * 1024
         ),
         name="blocks",
-    )(x_in.reshape(tiles, chans * rows, cols), w_reduce[0], w_spatial[0], w_expand[0],
-      gain_mid[0], bias_mid[0], gain_out.reshape(chans // mid, mid), bias_out.reshape(chans // mid, mid))
+    )(*(pltpu.with_memory_space_constraint(value, pltpu.HBM) for value in operands))
     return out.reshape(1, tiles, chans, rows, cols)
 
 

time: 50.9 us -> 34.3 us (0.67)
  Pallas kernels: 40.7 us -> 32.1 us
  local copies, waits for them, and re-layouts: 9.88 us -> 2.02 us
    pallas_call x1, Pallas kernels: 40.7 us -> 32.1 us  [on_device(): pl.pallas_call(functools.partial(kernel, levels, strips, rows), out_shape...]
    unnamed x17 -> x1, local copies, waits for them, and re-layouts: 9.88 us -> 2.02 us
where the time goes in v2:
time: 34.3 us; the launch traced here: 34.2 us
  Pallas kernels  32.1 us (94%)
  local copies, waits for them, and re-layouts  2.02 us (6%)
    pallas_call x1, Pallas kernels, on_device(): pl.pallas_call(functools.partial(kernel, levels, strips, rows), out_shape...  32.1 us
    unnamed x1, local copies, waits for them, and re-layouts  2.02 us

profile of v2, /device:TPU:19, one launch (start us, length us, event | category | flops | bytes accessed | tf_op | source)
XLA Modules:
  0.0 34.2 jit_solution(12342329452824001662)
XLA Ops:
  0.0 32.1 %blocks.1 = f32[4,2048,128]{2,1,0:T(8,128)S(1)} custom-call(f32[4,2048,128]{2,1,0:T(8,128)} %bitcast.10, f32[128,512]{1,0:T(8,128)} %bitcast.12, f32[9,128,128]{2,1,0:T(8,128)} %bitcast.11, f32[512,128]{1,0:T(8,128)} %bitcast.13, f32[2,128]{1,0:T(2,128)} %bitcast.16, f32[2,128]{1,0:T(2,128)} %bitcast.17, f32[4,128]{1,0:T(4,128)} %bitcast.14, f32[4,128]{1,0:T(4,128)} %bitcast.15), custom_call_target="tpu_custom_call" | custom-call | tf_op jit(solution)/shard_map/blocks/pallas_call | solution.py:318
  32.2 2.0 %copy.10 = f32[1,4,512,4,128]{4,3,2,1,0:T(4,128)} copy(f32[1,4,512,4,128]{4,3,2,1,0:T(4,128)S(1)} %bitcast.9) | data formatting | bytes 8388608

commit v3 on v2

--- a/solution.py
+++ b/solution.py
@@ -25,11 +25,11 @@
 
 
 def kernel(
-    levels, strips, rows,
+    levels, strips, groups, rows,
     x_ref, wr_ref, ws_ref, wx_ref, gm_ref, bm_ref, go_ref, bo_ref, cur,
     wr_all, ws_all, wx_all, pp_all, red, side, halo, relay,
     w_red, w_spa, w_exp, b_red, b_mid, b_out, sa, middle,
-    x_sem, own_sem, wsend, wrecv, rsend, rrecv, hsend, hrecv, nsend, nrecv, ysend, yrecv,
+    x_sem, own_sem, wsend, wrecv, gsend, grecv, rsend, rrecv, hsend, hrecv, nsend, nrecv, ysend, yrecv,
 ):
     tiles = x_ref.shape[0]
     chans = x_ref.shape[1] // rows
@@ -38,19 +38,24 @@
     strip = lax.axis_index("strip")
     sec = lax.axis_index("section")
     col = lax.axis_index("col")
+    grp = lax.axis_index("groups")
     other = {"col": 1 - col}
     srcs = (wr_ref, ws_ref, wx_ref)
     count = chans // mid
     terms = ((gm_ref, 0, 2), (bm_ref, 2, 2), (go_ref, 4, count), (bo_ref, 4 + count, count))
     slots = (wr_all, ws_all, wx_all, pp_all)
 
-    def share(kind, level, which):
-        if kind == 0:
-            return wr_all.at[level, pl.ds(which * (mid // 2), mid // 2), :]
-        if kind == 1:
-            return ws_all.at[level, :, pl.ds(which * (mid // 2), mid // 2), :]
-        if kind == 2:
-            return wx_all.at[level, pl.ds(which * (chans // 2), chans // 2), :]
+    def share(piece, level, which, of):
+        part = which * groups + of
+        if piece == 0:
+            size = mid // (2 * groups)
+            return wr_all.at[level, pl.ds(part * size, size), :]
+        if piece < 4:
+            size = mid // (2 * groups)
+            return ws_all.at[level, pl.ds(3 * (piece - 1), 3), pl.ds(part * size, size), :]
+        if piece == 4:
+            size = chans // (2 * groups)
+            return wx_all.at[level, pl.ds(part * size, size), :]
         return pp_all.at[level]
 
     def remote(src, dst, send, recv, device):
@@ -58,6 +63,42 @@
             src_ref=src, dst_ref=dst, send_sem=send, recv_sem=recv,
             device_id=device, device_id_type=pl.DeviceIdType.MESH,
         )
+
+    def across(piece, level, target):
+        part = share(piece, level, col, grp)
+        return remote(
+            part, part, wsend.at[piece, target], wrecv.at[piece, level], {"section": target}
+        )
+
+    def to_group(piece, level, step):
+        part = share(piece, level, col, grp)
+        return remote(
+            part, part, gsend.at[piece, level, step], grecv.at[piece, level, step],
+            {"groups": lax.rem(grp + step, groups)},
+        )
+
+    def to_core(piece, level, which, step):
+        part = share(piece, level, which, lax.rem(grp + groups - step, groups))
+        return remote(part, part, rsend.at[piece, level, step], rrecv.at[piece, level, step], other)
+
+    def forward(piece, level):
+        across(piece, level, 0).wait_recv()
+        if piece < 5:
+            for step in range(1, groups):
+                to_group(piece, level, step).start()
+            to_core(piece, level, col, 0).start()
+
+    def collect(piece, level):
+        for step in range(1, groups):
+            part = share(piece, level, col, lax.rem(grp + groups - step, groups))
+            remote(
+                part, part, gsend.at[piece, level, step], grecv.at[piece, level, step], other
+            ).wait_recv()
+            to_core(piece, level, col, step).start()
+
+    def complete(piece, level):
+        for step in range(groups):
+            to_core(piece, level, 1 - col, step).wait_recv()
 
     own = [
         pltpu.make_async_copy(srcs[k], slots[k].at[sec], own_sem.at[k]) for k in range(3)
@@ -90,17 +131,22 @@
                 barrier, inc=1, device_id={"strip": peer}, device_id_type=pl.DeviceIdType.MESH
             )
 
-    peers = levels + jnp.where(strip > 0, 1, 0) + jnp.where(strip < strips - 1, 1, 0)
+    for step in range(1, groups):
+        pl.semaphore_signal(
+            barrier, inc=1, device_id={"groups": lax.rem(grp + step, groups)},
+            device_id_type=pl.DeviceIdType.MESH,
+        )
+
+    peers = levels + groups - 1 + jnp.where(strip > 0, 1, 0) + jnp.where(strip < strips - 1, 1, 0)
     pl.semaphore_wait(barrier, peers)
 
-    for k in (3, 0, 1, 2):
-        for copy in own[3] if k == 3 else (own[k],):
+    for piece in (5, 0, 1, 2, 3, 4):
+        for copy in {5: own[3], 0: own[:1], 1: own[1:2], 4: own[2:3]}.get(piece, ()):
             copy.wait()
         for target in range(1, levels):
             @pl.when(sec < target)
-            def _(k=k, target=target):
-                part = share(k, sec, col)
-                remote(part, part, wsend.at[k, target], wrecv.at[k, sec], {"section": target}).start()
+            def _(piece=piece, target=target):
+                across(piece, sec, target).start()
 
     @pl.when(strip == 0)
     def _():
@@ -112,47 +158,49 @@
         halo[:, :, 1] = jnp.zeros(halo.shape[:2] + halo.shape[3:], F32)
         relay[:, :, 1] = jnp.zeros(relay.shape[:2] + relay.shape[3:], F32)
 
-    def relayed(k, level, which):
-        part = share(k, level, which)
-        return remote(part, part, rsend.at[k, level], rrecv.at[k, level], other)
-
-    def arrive(level, kinds):
-        @pl.when(sec > level)
-        def _():
-            for k in kinds:
-                part = share(k, level, col)
-                remote(part, part, wsend.at[k, 0], wrecv.at[k, level], other).wait_recv()
-                if k < 3:
-                    relayed(k, level, col).start()
-            for k in kinds:
-                if k < 3:
-                    relayed(k, level, 1 - col).wait_recv()
-
     def prepare_reduce(level):
-        arrive(level, (3, 0))
         gain = down_rows(pp_all[level, 0:1, :], mid)
-        for at in range(chans // mid):
+        for at in range(count):
             cut = slice(at * mid, (at + 1) * mid)
             high, low = split(wr_all[level, :, cut] * gain)
             w_red[level, 0:mid, cut] = high
             w_red[level, mid : 2 * mid, cut] = low
         b_red[level] = down_rows(pp_all[level, 2:3, :], mid)
 
-    def prepare_rest(level):
-        arrive(level, (1, 2))
+    def prepare_spatial(level):
         gain = down_rows(pp_all[level, 1:2, :], mid)
         for tap in range(9):
             high, low = split(ws_all[level, tap] * gain)
-            w_spa[0:mid, tap * mid : (tap + 1) * mid] = high
-            w_spa[mid : 2 * mid, tap * mid : (tap + 1) * mid] = low
-        b_mid[...] = down_rows(pp_all[level, 3:4, :], mid)
+            w_spa[level, 0:mid, tap * mid : (tap + 1) * mid] = high
+            w_spa[level, mid : 2 * mid, tap * mid : (tap + 1) * mid] = low
+        b_mid[level] = down_rows(pp_all[level, 3:4, :], mid)
+
+    def prepare_expand(level):
         for at in range(count):
             cut = slice(at * mid, (at + 1) * mid)
-            high, low = split(wx_all[level, cut, :] * down_rows(pp_all[level, 4 + at : 5 + at, :], mid))
-            w_exp[cut, 0:mid] = high
-            w_exp[cut, mid : 2 * mid] = high
-            w_exp[cut, 2 * mid : 3 * mid] = low
-            b_out[cut, :] = down_rows(pp_all[level, 4 + count + at : 5 + count + at, :], mid)
+            high, low = split(wx_all[level, cut, :] * down_rows(pp_all[level, pl.ds(4 + at, 1), :], mid))
+            w_exp[level, cut, 0:mid] = high
+            w_exp[level, cut, mid : 2 * mid] = high
+            w_exp[level, cut, 2 * mid : 3 * mid] = low
+            b_out[level, cut, :] = down_rows(pp_all[level, pl.ds(4 + count + at, 1), :], mid)
+
+    def arrive_reduce(level):
+        for piece in (5, 0, 1, 2):
+            forward(piece, level)
+        collect(0, level)
+        forward(3, level)
+        complete(0, level)
+        prepare_reduce(level)
+
+    def arrive_rest(level):
+        for piece in (1, 2, 3):
+            collect(piece, level)
+        for piece in (1, 2, 3):
+            complete(piece, level)
+        prepare_spatial(level)
+        collect(4, level)
+        complete(4, level)
+        prepare_expand(level)
 
     def to_strip(level, m, way):
         return remote(
@@ -236,37 +284,57 @@
             )
             for first in (0, 3 * mid)
         )
-        both = dot(w_spa[...], high)
-        total = both[:mid] + both[mid:] + dot(w_spa[0:mid, :], low)
-        total = jnp.maximum(total + jnp.concatenate([b_mid[...]] * rows, axis=1), 0.0)
+        both = dot(w_spa[level], high)
+        total = both[:mid] + both[mid:] + dot(w_spa[level, 0:mid, :], low)
+        total = jnp.maximum(total + jnp.concatenate([b_mid[level]] * rows, axis=1), 0.0)
         high, low = split(total)
         middle[0:mid, :] = high
         middle[mid : 2 * mid, :] = low
         for pair in range(rows // 2):
             lanes = slice(2 * pair * cols, (2 * pair + 2) * cols)
             high, low = middle[0:mid, lanes], middle[mid : 2 * mid, lanes]
-            grown = dot(w_exp[...], jnp.concatenate([high, low, high], axis=0))
+            grown = dot(w_exp[level], jnp.concatenate([high, low, high], axis=0))
             for j in range(2):
                 at = pl.ds(2 * pair + j, chans, stride=rows)
                 cur.at[m][at, :] = jnp.maximum(
-                    cur.at[m][at, :] + grown[:, j * cols : (j + 1) * cols] + b_out[...], 0.0
+                    cur.at[m][at, :] + grown[:, j * cols : (j + 1) * cols] + b_out[level], 0.0
                 )
 
-    prepare_reduce(0)
+    prepare_reduce(sec)
+
+    @pl.when(sec > 0)
+    def _():
+        prepare_spatial(sec)
+        prepare_expand(sec)
+        arrive_reduce(0)
 
     @pl.loop(0, tiles)
     def _(m):
         pltpu.make_async_copy(x_ref.at[m], cur.at[m], x_sem.at[m]).wait()
         reduce_tile(0, m)
 
+        @pl.when((sec > 0) & (m == 0))
+        def _():
+            forward(4, 0)
+
+    @pl.when(sec == 0)
+    def _():
+        prepare_spatial(0)
+        prepare_expand(0)
+
     for level in range(levels):
         @pl.when(sec >= level)
         def _(level=level):
-            prepare_rest(level)
+            @pl.when(sec > level)
+            def _():
+                if level > 0:
+                    forward(4, level)
+                arrive_rest(level)
+
             if level + 1 < levels:
-                @pl.when(sec > level)
+                @pl.when(sec > level + 1)
                 def _():
-                    prepare_reduce(level + 1)
+                    arrive_reduce(level + 1)
 
             take_halo(level, 0)
 
@@ -294,20 +362,22 @@
                     def _(way=way):
                         pass_on(level, m, way).wait_send()
 
-    for k in range(4):
+    for piece in range(6):
         for target in range(1, levels):
             @pl.when(sec < target)
-            def _(k=k, target=target):
-                part = share(k, sec, col)
-                remote(part, part, wsend.at[k, target], wrecv.at[k, sec], {"section": target}).wait_send()
-        if k < 3:
+            def _(piece=piece, target=target):
+                across(piece, sec, target).wait_send()
+        if piece < 5:
             for level in range(levels - 1):
                 @pl.when(sec > level)
-                def _(k=k, level=level):
-                    relayed(k, level, col).wait_send()
-
-
-def on_device(levels, strips, x_in, w_reduce, w_spatial, w_expand, gain_mid, bias_mid, gain_out, bias_out):
+                def _(piece=piece, level=level):
+                    for step in range(1, groups):
+                        to_group(piece, level, step).wait_send()
+                    for step in range(groups):
+                        to_core(piece, level, col, step).wait_send()
+
+
+def on_device(levels, strips, groups, x_in, w_reduce, w_spatial, w_expand, gain_mid, bias_mid, gain_out, bias_out):
     tiles, chans, rows, cols = x_in.shape
     mid = w_reduce.shape[1]
     operands = (
@@ -316,7 +386,7 @@
     )
     dma = pltpu.SemaphoreType.DMA
     out = pl.pallas_call(
-        functools.partial(kernel, levels, strips, rows),
+        functools.partial(kernel, levels, strips, groups, rows),
         out_shape=jax.ShapeDtypeStruct((tiles, chans * rows, cols), F32),
         in_specs=[pl.BlockSpec(memory_space=pltpu.HBM)] * 8,
         out_specs=pl.BlockSpec(memory_space=pltpu.VMEM),
@@ -330,19 +400,21 @@
             pltpu.VMEM((levels, tiles, 2, mid, cols), F32),
             pltpu.VMEM((levels, tiles, 2, mid, cols), F32),
             pltpu.VMEM((levels, 2 * mid, chans), BF),
-            pltpu.VMEM((2 * mid, 9 * mid), BF),
-            pltpu.VMEM((chans, 3 * mid), BF),
+            pltpu.VMEM((levels, 2 * mid, 9 * mid), BF),
+            pltpu.VMEM((levels, chans, 3 * mid), BF),
             pltpu.VMEM((levels, mid, cols), F32),
-            pltpu.VMEM((mid, cols), F32),
-            pltpu.VMEM((chans, cols), F32),
+            pltpu.VMEM((levels, mid, cols), F32),
+            pltpu.VMEM((levels, chans, cols), F32),
             pltpu.VMEM((6 * mid, (rows + 2) * cols), BF),
             pltpu.VMEM((2 * mid, rows * cols), BF),
             dma((tiles,)),
             dma((7,)),
-            dma((4, levels)),
-            dma((4, levels)),
-            dma((3, levels)),
-            dma((3, levels)),
+            dma((6, levels)),
+            dma((6, levels)),
+            dma((5, levels, groups)),
+            dma((5, levels, groups)),
+            dma((5, levels, groups)),
+            dma((5, levels, groups)),
             dma((levels, tiles, 2)),
             dma((levels, tiles, 2)),
             dma((levels, tiles)),
@@ -371,6 +443,6 @@
     )
     out_specs = P("section", "groups", None, "strip", "col")
     return jax.shard_map(
-        functools.partial(on_device, mesh.shape["section"], mesh.shape["strip"]),
+        functools.partial(on_device, mesh.shape["section"], mesh.shape["strip"], mesh.shape["groups"]),
         mesh=mesh, in_specs=in_specs, out_specs=out_specs, check_vma=False,
     )

time: 34.3 us -> 33.8 us (0.985)
  Pallas kernels: 32.1 us -> 31.6 us
    pallas_call x1, Pallas kernels: 32.1 us -> 31.6 us  [on_device(): pl.pallas_call(functools.partial(kernel, levels, strips, groups, rows), o...]
where the time goes in v3:
time: 33.8 us; the launch traced here: 33.7 us
  Pallas kernels  31.6 us (93%)
  local copies, waits for them, and re-layouts  2.02 us (6%)
    pallas_call x1, Pallas kernels, on_device(): pl.pallas_call(functools.partial(kernel, levels, strips, groups, rows), o...  31.6 us
    unnamed x1, local copies, waits for them, and re-layouts  2.02 us

profile of v3, /device:TPU:19, one launch (start us, length us, event | category | flops | bytes accessed | tf_op | source)
XLA Modules:
  0.0 33.7 jit_solution(10343282191316704839)
XLA Ops:
  0.0 31.6 %blocks.1 = f32[4,2048,128]{2,1,0:T(8,128)S(1)} custom-call(f32[4,2048,128]{2,1,0:T(8,128)} %bitcast.10, f32[128,512]{1,0:T(8,128)} %bitcast.12, f32[9,128,128]{2,1,0:T(8,128)} %bitcast.11, f32[512,128]{1,0:T(8,128)} %bitcast.13, f32[2,128]{1,0:T(2,128)} %bitcast.16, f32[2,128]{1,0:T(2,128)} %bitcast.17, f32[4,128]{1,0:T(4,128)} %bitcast.14, f32[4,128]{1,0:T(4,128)} %bitcast.15), custom_call_target="tpu_custom_call" | custom-call | tf_op jit(solution)/shard_map/blocks/pallas_call | solution.py:388
  31.6 2.0 %copy.10 = f32[1,4,512,4,128]{4,3,2,1,0:T(4,128)} copy(f32[1,4,512,4,128]{4,3,2,1,0:T(4,128)S(1)} %bitcast.9) | data formatting | bytes 8388608

commit v4 on v3

--- a/solution.py
+++ b/solution.py
@@ -27,7 +27,7 @@
 def kernel(
     levels, strips, groups, rows,
     x_ref, wr_ref, ws_ref, wx_ref, gm_ref, bm_ref, go_ref, bo_ref, cur,
-    wr_all, ws_all, wx_all, pp_all, red, side, halo, relay,
+    wr_all, ws_all, wx_all, pp_all, red, edges, side, halo, corner, relay,
     w_red, w_spa, w_exp, b_red, b_mid, b_out, sa, middle,
     x_sem, own_sem, wsend, wrecv, gsend, grecv, rsend, rrecv, hsend, hrecv, nsend, nrecv, ysend, yrecv,
 ):
@@ -151,12 +151,10 @@
     @pl.when(strip == 0)
     def _():
         halo[:, :, 0] = jnp.zeros(halo.shape[:2] + halo.shape[3:], F32)
-        relay[:, :, 0] = jnp.zeros(relay.shape[:2] + relay.shape[3:], F32)
 
     @pl.when(strip == strips - 1)
     def _():
         halo[:, :, 1] = jnp.zeros(halo.shape[:2] + halo.shape[3:], F32)
-        relay[:, :, 1] = jnp.zeros(relay.shape[:2] + relay.shape[3:], F32)
 
     def prepare_reduce(level):
         gain = down_rows(pp_all[level, 0:1, :], mid)
@@ -210,13 +208,22 @@
         )
 
     def to_side(level, m):
-        return remote(red.at[level, m], side.at[level, m], nsend.at[level, m], nrecv.at[level, m], other)
-
-    def pass_on(level, m, way):
-        return remote(
-            halo.at[level, m, way], relay.at[level, m, way],
-            ysend.at[level, m, way], yrecv.at[level, m, way], other,
-        )
+        return remote(edges.at[level, m], side.at[level, m], nsend.at[level, m], nrecv.at[level, m], other)
+
+    def pass_on(level, m):
+        return remote(corner.at[level, m], relay.at[level, m], ysend.at[level, m], yrecv.at[level, m], other)
+
+    lane = lax.broadcasted_iota(jnp.int32, (mid, cols), 1)
+    on_edge = lane == jnp.where(col == 0, cols - 1, 0)
+
+    def pack(values):
+        total = jnp.where(on_edge, values[0], 0.0)
+        for step, value in enumerate(values[1:], 1):
+            total = total + pltpu.roll(jnp.where(on_edge, value, 0.0), step, 1)
+        return total
+
+    def unpack(value, step):
+        return pltpu.roll(value, cols - step, 1) if step else value
 
     has = (strip > 0, strip < strips - 1)
 
@@ -242,6 +249,7 @@
         def _():
             to_strip(level, m, 1).start()
 
+        edges[level, m] = pack([red[level, m, at] for at in range(rows)])
         to_side(level, m).start()
 
     def take_halo(level, m):
@@ -249,9 +257,10 @@
             @pl.when(has[way])
             def _(way=way):
                 to_strip(level, m, way).wait_recv()
-                pass_on(level, m, way).start()
-
-    lane = lax.broadcasted_iota(jnp.int32, (mid, cols), 1)
+
+        corner[level, m] = pack([halo[level, m, 0], halo[level, m, 1]])
+        pass_on(level, m).start()
+
     left_edge = lane == cols - 1
     right_edge = lane == 0
     left_on = jnp.where(col == 1, 1.0, 0.0).astype(F32)
@@ -259,17 +268,14 @@
 
     def finish_tile(level, m):
         to_side(level, m).wait_recv()
-        for way in range(2):
-            @pl.when(has[way])
-            def _(way=way):
-                pass_on(level, m, way).wait_recv()
+        pass_on(level, m).wait_recv()
         for at in range(rows + 2):
             if at == 0:
-                centre, beside = halo[level, m, 0], relay[level, m, 0]
+                centre, beside = halo[level, m, 0], relay[level, m]
             elif at == rows + 1:
-                centre, beside = halo[level, m, 1], relay[level, m, 1]
+                centre, beside = halo[level, m, 1], unpack(relay[level, m], 1)
             else:
-                centre, beside = red[level, m, at - 1], side[level, m, at - 1]
+                centre, beside = red[level, m, at - 1], unpack(side[level, m], at - 1)
             lanes = slice(at * cols, (at + 1) * cols)
             left = pltpu.roll(jnp.where(left_edge, beside * left_on, centre), 1, 1)
             right = pltpu.roll(jnp.where(right_edge, beside * right_on, centre), cols - 1, 1)
@@ -353,14 +359,11 @@
             @pl.loop(0, tiles)
             def _(m):
                 to_side(level, m).wait_send()
+                pass_on(level, m).wait_send()
                 for way in range(2):
                     @pl.when(has[1 - way])
                     def _(way=way):
                         to_strip(level, m, way).wait_send()
-
-                    @pl.when(has[way])
-                    def _(way=way):
-                        pass_on(level, m, way).wait_send()
 
     for piece in range(6):
         for target in range(1, levels):
@@ -396,9 +399,11 @@
             pltpu.VMEM((levels, chans, mid), F32),
             pltpu.VMEM((levels, 4 + 2 * (chans // mid), mid), F32),
             pltpu.VMEM((levels, tiles, rows, mid, cols), F32),
-            pltpu.VMEM((levels, tiles, rows, mid, cols), F32),
+            pltpu.VMEM((levels, tiles, mid, cols), F32),
+            pltpu.VMEM((levels, tiles, mid, cols), F32),
             pltpu.VMEM((levels, tiles, 2, mid, cols), F32),
-            pltpu.VMEM((levels, tiles, 2, mid, cols), F32),
+            pltpu.VMEM((levels, tiles, mid, cols), F32),
+            pltpu.VMEM((levels, tiles, mid, cols), F32),
             pltpu.VMEM((levels, 2 * mid, chans), BF),
             pltpu.VMEM((levels, 2 * mid, 9 * mid), BF),
             pltpu.VMEM((levels, chans, 3 * mid), BF),
@@ -419,8 +424,8 @@
             dma((levels, tiles, 2)),
             dma((levels, tiles)),
             dma((levels, tiles)),
-            dma((levels, tiles, 2)),
-            dma((levels, tiles, 2)),
+            dma((levels, tiles)),
+            dma((levels, tiles)),
         ],
         compiler_params=pltpu.CompilerParams(
             collective_id=0, has_side_effects=True, vmem_limit_bytes=40 * 1024 * 1024

time: 33.8 us -> 34.9 us (1.033)
  Pallas kernels: 31.6 us -> 32.7 us
    pallas_call x1, Pallas kernels: 31.6 us -> 32.7 us  [on_device(): pl.pallas_call(functools.partial(kernel, levels, strips, groups, rows), o...]
where the time goes in v4:
time: 34.9 us; the launch traced here: 34.7 us
  Pallas kernels  32.7 us (94%)
  local copies, waits for them, and re-layouts  2.02 us (6%)
    pallas_call x1, Pallas kernels, on_device(): pl.pallas_call(functools.partial(kernel, levels, strips, groups, rows), o...  32.7 us
    unnamed x1, local copies, waits for them, and re-layouts  2.02 us

profile of v4, /device:TPU:19, one launch (start us, length us, event | category | flops | bytes accessed | tf_op | source)
XLA Modules:
  0.0 34.7 jit_solution(5634249139276977466)
XLA Ops:
  0.0 32.7 %blocks.1 = f32[4,2048,128]{2,1,0:T(8,128)S(1)} custom-call(f32[4,2048,128]{2,1,0:T(8,128)} %bitcast.10, f32[128,512]{1,0:T(8,128)} %bitcast.12, f32[9,128,128]{2,1,0:T(8,128)} %bitcast.11, f32[512,128]{1,0:T(8,128)} %bitcast.13, f32[2,128]{1,0:T(2,128)} %bitcast.16, f32[2,128]{1,0:T(2,128)} %bitcast.17, f32[4,128]{1,0:T(4,128)} %bitcast.14, f32[4,128]{1,0:T(4,128)} %bitcast.15), custom_call_target="tpu_custom_call" | custom-call | tf_op jit(solution)/shard_map/blocks/pallas_call | solution.py:391
  32.7 2.0 %copy.10 = f32[1,4,512,4,128]{4,3,2,1,0:T(4,128)} copy(f32[1,4,512,4,128]{4,3,2,1,0:T(4,128)S(1)} %bitcast.9) | data formatting | bytes 8388608

commit v5 on v3

--- a/solution.py
+++ b/solution.py
@@ -290,6 +290,11 @@
         high, low = split(total)
         middle[0:mid, :] = high
         middle[mid : 2 * mid, :] = low
+
+        @pl.when(m + 1 < tiles)
+        def _():
+            take_halo(level, m + 1)
+
         for pair in range(rows // 2):
             lanes = slice(2 * pair * cols, (2 * pair + 2) * cols)
             high, low = middle[0:mid, lanes], middle[mid : 2 * mid, lanes]
@@ -340,10 +345,6 @@
 
             @pl.loop(0, tiles)
             def _(m):
-                @pl.when(m + 1 < tiles)
-                def _():
-                    take_halo(level, m + 1)
-
                 finish_tile(level, m)
                 if level + 1 < levels:
                     @pl.when(sec > level)

time: 33.8 us -> 36.6 us (1.083)
  Pallas kernels: 31.6 us -> 34.4 us
    pallas_call x1, Pallas kernels: 31.6 us -> 34.4 us  [on_device(): pl.pallas_call(functools.partial(kernel, levels, strips, groups, rows), o...]
where the time goes in v5:
time: 36.6 us; the launch traced here: 36.5 us
  Pallas kernels  34.4 us (94%)
  local copies, waits for them, and re-layouts  2.02 us (6%)
    pallas_call x1, Pallas kernels, on_device(): pl.pallas_call(functools.partial(kernel, levels, strips, groups, rows), o...  34.4 us
    unnamed x1, local copies, waits for them, and re-layouts  2.02 us

profile of v5, /device:TPU:19, one launch (start us, length us, event | category | flops | bytes accessed | tf_op | source)
XLA Modules:
  0.0 36.5 jit_solution(3889914612458104707)
XLA Ops:
  0.0 34.4 %blocks.1 = f32[4,2048,128]{2,1,0:T(8,128)S(1)} custom-call(f32[4,2048,128]{2,1,0:T(8,128)} %bitcast.10, f32[128,512]{1,0:T(8,128)} %bitcast.12, f32[9,128,128]{2,1,0:T(8,128)} %bitcast.11, f32[512,128]{1,0:T(8,128)} %bitcast.13, f32[2,128]{1,0:T(2,128)} %bitcast.16, f32[2,128]{1,0:T(2,128)} %bitcast.17, f32[4,128]{1,0:T(4,128)} %bitcast.14, f32[4,128]{1,0:T(4,128)} %bitcast.15), custom_call_target="tpu_custom_call" | custom-call | tf_op jit(solution)/shard_map/blocks/pallas_call | solution.py:389
  34.5 2.0 %copy.10 = f32[1,4,512,4,128]{4,3,2,1,0:T(4,128)} copy(f32[1,4,512,4,128]{4,3,2,1,0:T(4,128)S(1)} %bitcast.9) | data formatting | bytes 8388608
